TPU v7x, 32 devices: a whole 2x2x4 slice. The times are simulated.
32 devices in a mesh: expert: 8 (over z, core), tensor: 4 (over y, x).
Axes of the slice: x: 2, y: 2, z: 4, core: 2. Of those that a mesh axis runs over, the one named last changes fastest.
Arguments:
- tokens: bfloat16 [256, 4096], P('expert', 'tensor'), may hold values from -6 to 6
- cotangent: bfloat16 [256, 4096], P('expert', 'tensor'), may hold values from -6 to 6
- expert_ids: int32 [256, 8], P('expert'), may hold values from 0 to 63, all different within a row; in each aligned block of 32 rows (0 to 31, 32 to 63, ...) at most 8 rows name the same one
- route_weight: float32 [256, 8], P('expert'), may hold values from 0.05 to 0.25
- w_gate: bfloat16 [64, 4096, 1536], P('expert', 'tensor'), may hold values from -0.09375 to 0.09375
- w_up: bfloat16 [64, 4096, 1536], P('expert', 'tensor'), may hold values from -0.09375 to 0.09375
- w_down: bfloat16 [64, 1536, 4096], P('expert', None, 'tensor'), may hold values from -0.15625 to 0.15625
Outputs:
- mixed_out: bfloat16 [256, 4096], P('expert', 'tensor')
- input_grad: bfloat16 [256, 4096], P('expert', 'tensor')
- down_grad: bfloat16 [64, 1536, 4096], P('expert', None, 'tensor')
Inputs may be any that keep to these rules, and one draw needn't show every extreme that they name: `expert_ids`: each row names 8 different experts; within the 32 rows of one device no expert is named more than 8 times.
All inputs are finite; a program needn't handle non-finite values.
Results may differ from a plain program's by a relative error of at most 0.023.
Values may be sent and summed in bfloat16 or wider, within the bound.
No kernel may reach another device: no remote copies, remote signals or barrier semaphores. Data moves between devices by JAX's collectives and lax.ppermute only.
A program may use at most 192 MiB of HBM per device.

v0:
```python
import jax
import jax.numpy as jnp
from jax import lax
from jax.sharding import PartitionSpec as P


def local(tokens, cotangent, expert_ids, route_weight, w_gate, w_up, w_down):
    resident_specialists = w_gate.shape[0]
    experts = resident_specialists * lax.axis_size("expert")
    tok_count = expert_ids.shape[0]
    top_count = expert_ids.shape[1]
    capacity = 2 * tok_count * top_count // experts
    model_width = tokens.shape[1]
    flat_ids = expert_ids.reshape(-1)
    onehot = (flat_ids[:, None] == jnp.arange(experts, dtype=jnp.int32)[None, :]).astype(jnp.int32)
    before = jnp.cumsum(onehot, axis=0) - onehot
    slot_index = jnp.sum(before * onehot, axis=1)
    target = flat_ids * capacity + slot_index
    chosen = (target[:, None] == jnp.arange(experts * capacity, dtype=jnp.int32)[None, :]).astype(
        jnp.float32
    )
    chosen = chosen.reshape(tok_count, top_count, experts * capacity)
    expert_assignment = jnp.sum(chosen, axis=1)
    weighted = jnp.sum(chosen * route_weight[:, :, None], axis=1)
    token_send = jnp.dot(
        expert_assignment.T.astype(jnp.bfloat16), tokens, preferred_element_type=jnp.float32
    )
    token_send = token_send.astype(jnp.bfloat16).reshape(experts, capacity, model_width)
    gradient_outgoing = jnp.dot(
        weighted.T, cotangent, precision=lax.Precision.HIGHEST, preferred_element_type=jnp.float32
    )
    gradient_outgoing = gradient_outgoing.astype(jnp.bfloat16).reshape(
        experts, capacity, model_width
    )
    token_rows, grad_rows = (
        lax.all_to_all(token_send, "expert", split_axis=0, concat_axis=1, tiled=True),
        lax.all_to_all(gradient_outgoing, "expert", split_axis=0, concat_axis=1, tiled=True),
    )
    pre_gate = jnp.einsum("erd,edf->erf", token_rows, w_gate, preferred_element_type=jnp.float32)
    pre_up = jnp.einsum("erd,edf->erf", token_rows, w_up, preferred_element_type=jnp.float32)
    slice_breadth = w_gate.shape[2] // lax.axis_size("tensor")
    gate_sum, up_sum = (
        lax.psum(pre_gate.astype(jnp.bfloat16), "tensor").astype(jnp.float32),
        lax.psum(pre_up.astype(jnp.bfloat16), "tensor").astype(jnp.float32),
    )
    sigmoid_all = jax.nn.sigmoid(gate_sum)
    hidden = (gate_sum * sigmoid_all * up_sum).astype(jnp.bfloat16)
    out_rows = jnp.einsum(
        "erf,efd->erd", hidden, w_down, preferred_element_type=jnp.float32
    ).astype(jnp.bfloat16)
    down_grad = jnp.einsum("erf,erd->efd", hidden, grad_rows, preferred_element_type=jnp.float32)
    offset = lax.axis_index("tensor") * slice_breadth
    gate_part = lax.dynamic_slice_in_dim(gate_sum, offset, slice_breadth, 2)
    up_part = lax.dynamic_slice_in_dim(up_sum, offset, slice_breadth, 2)
    sigmoid_part = lax.dynamic_slice_in_dim(sigmoid_all, offset, slice_breadth, 2)
    hidden_term = jnp.einsum("erd,efd->erf", grad_rows, w_down, preferred_element_type=jnp.float32)
    hidden_grad = lax.psum_scatter(
        hidden_term.astype(jnp.bfloat16), "tensor", scatter_dimension=2, tiled=True
    ).astype(jnp.float32)
    gate_grad = (
        hidden_grad * up_part * sigmoid_part * (1.0 + gate_part * (1.0 - sigmoid_part))
    ).astype(jnp.bfloat16)
    up_grad = (hidden_grad * gate_part * sigmoid_part).astype(jnp.bfloat16)
    gate_piece = lax.all_gather(gate_grad, "tensor", axis=2, tiled=True)
    up_piece = lax.all_gather(up_grad, "tensor", axis=2, tiled=True)
    running = jnp.einsum("erf,edf->erd", gate_piece, w_gate, preferred_element_type=jnp.float32)
    input_rows = running + jnp.einsum(
        "erf,edf->erd", up_piece, w_up, preferred_element_type=jnp.float32
    )
    input_rows = input_rows.astype(jnp.bfloat16)
    returned_out, returned_in = (
        lax.all_to_all(out_rows, "expert", split_axis=1, concat_axis=0, tiled=True),
        lax.all_to_all(input_rows, "expert", split_axis=1, concat_axis=0, tiled=True),
    )
    returned_out = returned_out.reshape(experts * capacity, model_width)
    returned_in = returned_in.reshape(experts * capacity, model_width)
    mixed_out = jnp.dot(
        weighted, returned_out, precision=lax.Precision.HIGHEST, preferred_element_type=jnp.float32
    )
    input_grad = jnp.dot(
        expert_assignment.astype(jnp.bfloat16), returned_in, preferred_element_type=jnp.float32
    )
    return (
        mixed_out.astype(jnp.bfloat16),
        input_grad.astype(jnp.bfloat16),
        down_grad.astype(jnp.bfloat16),
    )


def solution(mesh):
    return jax.shard_map(
        local,
        mesh=mesh,
        in_specs=(
            P("expert", "tensor"),
            P("expert", "tensor"),
            P("expert", None),
            P("expert", None),
            P("expert", "tensor", None),
            P("expert", "tensor", None),
            P("expert", None, "tensor"),
        ),
        out_specs=(P("expert", "tensor"), P("expert", "tensor"), P("expert", None, "tensor")),
        check_vma=False,
    )
```

profile of v0, /device:TPU:0, one launch (start us, length us, event | category | flops | bytes accessed | tf_op | source)
XLA Modules:
  0.0 326.9 jit_solution(5938493697258200641)
XLA Ops:
  7.2 0.8 copy.45
  8.0 0.1 eq.43
  8.1 0.1 eq.39
  8.2 0.8 copy.49
  8.9 0.6 reduce-window.6
  9.6 0.2 slice_reduce_fusion
  9.8 0.1 fusion.17
  9.9 0.1 reduce_sum.30
  10.0 0.4 convert_reduce_fusion
  10.4 0.6 copy-done.4
  11.0 1.4 fusion
  12.4 6.4 %all-to-all-start = ((bf16[64,8,1024]{2,1,0:T(8,128)(2,1)}), bf16[64,8,1024]{2,1,0:T(8,128)(2,1)S(1)}, u32[]{:S(2)}, u32[]{:S(2)}) async-start(bf16[64,8,1024]{2,1,0:T(8,128)(2,1)} %fusion), calls=%async_computation | async-start | bytes 2097152 | tf_op jit(solution)/shard_map/all_to_all | solution.py:36
  18.8 2.0 fusion.1
  20.8 24.5 %all-to-all-done = bf16[64,8,1024]{2,1,0:T(8,128)(2,1)S(1)} async-done(((bf16[64,8,1024]{2,1,0:T(8,128)(2,1)}), bf16[64,8,1024]{2,1,0:T(8,128)(2,1)S(1)}, u32[]{:S(2)}, u32[]{:S(2)}) %all-to-all-start) | async-done | bytes 1048608 | tf_op jit(solution)/shard_map/all_to_all | solution.py:36
  45.4 3.6 %all-to-all-start.2 = ((bf16[64,8,1024]{2,1,0:T(8,128)(2,1)}), bf16[64,8,1024]{2,1,0:T(8,128)(2,1)S(1)}, u32[]{:S(2)}, u32[]{:S(2)}) async-start(bf16[64,8,1024]{2,1,0:T(8,128)(2,1)} %fusion.1), calls=%async_computation.2 | async-start | bytes 2097152 | tf_op jit(solution)/shard_map/all_to_all | solution.py:37
  48.9 0.0 all-reduce.3.cloned.1.call-start
  49.0 13.7 %convolution_convert_fusion.2 = bf16[8,64,1536]{2,1,0:T(8,128)(2,1)} fusion(bf16[8,1024,1536]{2,1,0:T(8,128)(2,1)} %param.12, bf16[8,8,8,1024]{3,2,1,0:T(8,128)(2,1)S(1)} %bitcast.68), kind=kOutput, calls=%fused_computation.4 | convolution fusion | flops 1611399168 | bytes 27787264 | tf_op jit(solution)/shard_map/erd,edf->erf/dot_general | solution.py:40
  62.7 13.7 %convolution_convert_fusion.3 = bf16[8,64,1536]{2,1,0:T(8,128)(2,1)} fusion(bf16[8,1024,1536]{2,1,0:T(8,128)(2,1)} %param.11, bf16[8,8,8,1024]{3,2,1,0:T(8,128)(2,1)S(1)} %bitcast.69), kind=kOutput, calls=%fused_computation.5 | convolution fusion | flops 1611399168 | bytes 27787264 | tf_op jit(solution)/shard_map/erd,edf->erf/dot_general | solution.py:39
  76.4 0.0 reduce-scatter.4.cloned.1.call-start
  76.5 13.2 %convolution_convert_fusion.1 = bf16[8,64,1536]{2,1,0:T(8,128)(2,1)S(1)} fusion(bf16[8,1536,1024]{2,1,0:T(8,128)(2,1)} %param.13, bf16[8,8,8,1024]{3,2,1,0:T(8,128)(2,1)S(1)} %bitcast.65), kind=kOutput, calls=%fused_computation.3 | convolution fusion | flops 1611399168 | bytes 27787264 | tf_op jit(solution)/shard_map/erd,efd->erf/dot_general | solution.py:56
  89.7 3.5 %copy.60 = bf16[8,64,1536]{1,0,2:T(8,128)(2,1)} copy(bf16[8,64,1536]{2,1,0:T(8,128)(2,1)S(1)} %convolution_convert_fusion.1) | data formatting | bytes 3145728
  93.2 5.4 %reshape.61 = bf16[1536,512]{1,0:T(8,128)(2,1)} reshape(bf16[1536,8,64]{2,1,0:T(8,128)(2,1)} %bitcast.67) | data formatting | bytes 3145728
  98.6 0.2 all-gather.3.cloned.1.call-start
  98.9 66.0 %all-reduce.3.cloned.1.call-done = (bf16[8,64,1536]{2,1,0:T(8,128)(2,1)}, bf16[8,64,1536]{2,1,0:T(8,128)(2,1)}) async-done(((bf16[8,64,1536]{2,1,0:T(8,128)(2,1)}, bf16[8,64,1536]{2,1,0:T(8,128)(2,1)}), (bf16[8,64,1536]{2,1,0:T(8,128)(2,1)}, bf16[8,64,1536]{2,1,0:T(8,128)(2,1)})) %all-reduce.3.cloned.1.call-update) | async-done | bytes 3145744 | tf_op jit(solution)/shard_map/psum | solution.py:43
  164.9 3.6 %convert_element_type.70 = f32[8,64,1536]{2,1,0:T(8,128)} convert(bf16[8,64,1536]{2,1,0:T(8,128)(2,1)} %get-tuple-element.5) | non-fusion elementwise | flops 786432 | bytes 4718592 | tf_op jit(solution)/shard_map/convert_element_type | solution.py:43
  168.5 2.5 add_divide_fusion
  171.0 28.1 %reduce-scatter.4.cloned.1.call-done = bf16[384,512]{1,0:T(8,128)(2,1)} async-done(((bf16[1536,512]{1,0:T(8,128)(2,1)}), bf16[384,512]{1,0:T(8,128)(2,1)}) %reduce-scatter.4.cloned.1.call-update) | async-done | bytes 393232
  199.0 1.5 reshape.62
  200.6 1.3 copy.61
  201.8 1.8 convert_element_type.72
  203.7 2.6 fusion.14
  206.3 0.0 all-gather.5.cloned.1.call-start
  206.4 0.5 all-gather.5.cloned.1.call-update
  206.9 13.5 %convolution_convert_fusion.4 = bf16[8,64,1024]{2,1,0:T(8,128)(2,1)S(1)} fusion(bf16[8,1536,1024]{2,1,0:T(8,128)(2,1)} %param.13, bf16[8,64,1536]{2,1,0:T(8,128)(2,1)S(1)} %copy-done.2, bf16[8,64,1536]{2,1,0:T(8,128)(2,1)} %get-tuple-element.6), kind=kOutput, calls=%fused_computation.7 | convolution fusion | flops 1617428480 | bytes 29360128 | tf_op jit(solution)/shard_map/erf,efd->erd/dot_general | solution.py:48
  220.4 1.6 copy.51
  222.0 4.6 %all-to-all-start.1 = ((bf16[8,64,1024]{2,0,1:T(8,128)(2,1)}), bf16[8,64,1024]{2,0,1:T(8,128)(2,1)}, u32[]{:S(2)}, u32[]{:S(2)}) async-start(bf16[8,64,1024]{2,0,1:T(8,128)(2,1)} %copy.51), calls=%async_computation.1 | async-start | bytes 2097152 | tf_op jit(solution)/shard_map/all_to_all | solution.py:72
  226.6 10.6 %all-gather.3.cloned.1.call-done = bf16[8,64,1536]{2,1,0:T(8,128)(2,1)} async-done(((bf16[8,64,384]{2,1,0:T(8,128)(2,1)}), bf16[8,64,1536]{2,1,0:T(8,128)(2,1)}) %all-gather.3.cloned.1.call-update) | async-done | bytes 1572880 | tf_op jit(solution)/shard_map/all_gather | solution.py:64
  237.2 13.8 %fusion.21 = f32[8,64,1024]{2,1,0:T(8,128)} fusion(bf16[8,64,1536]{2,1,0:T(8,128)(2,1)} %all-gather.3.cloned.1.call-done, bf16[8,1024,1536]{2,1,0:T(8,128)(2,1)} %param.11), kind=kOutput, calls=%fused_computation.44 | convolution fusion | flops 1610612736 | bytes 28835840 | tf_op jit(solution)/shard_map/erf,edf->erd/dot_general | solution.py:66
  251.0 18.6 %all-gather.5.cloned.1.call-done = bf16[8,64,1536]{2,1,0:T(8,128)(2,1)} async-done(((bf16[8,64,384]{2,1,0:T(8,128)(2,1)}), bf16[8,64,1536]{2,1,0:T(8,128)(2,1)}) %all-gather.5.cloned.1.call-update) | async-done | bytes 1572880 | tf_op jit(solution)/shard_map/all_gather | solution.py:65
  269.6 14.0 %add_convert_fusion = bf16[8,64,1024]{2,1,0:T(8,128)(2,1)} fusion(f32[8,64,1024]{2,1,0:T(8,128)} %fusion.21, bf16[8,64,1536]{2,1,0:T(8,128)(2,1)} %all-gather.5.cloned.1.call-done, bf16[8,1024,1536]{2,1,0:T(8,128)(2,1)} %param.12), kind=kOutput, calls=%fused_computation.6 | convolution fusion | flops 1611661312 | bytes 29884416 | tf_op jit(solution)/shard_map/erf,edf->erd/dot_general | solution.py:67
  283.6 2.8 copy.55
  286.3 4.6 %all-to-all-start.3 = ((bf16[8,64,1024]{2,0,1:T(8,128)(2,1)}), bf16[8,64,1024]{2,0,1:T(8,128)(2,1)}, u32[]{:S(2)}, u32[]{:S(2)}) async-start(bf16[8,64,1024]{2,0,1:T(8,128)(2,1)} %copy.55), calls=%async_computation.3 | async-start | bytes 2097152 | tf_op jit(solution)/shard_map/all_to_all | solution.py:73
  291.0 13.8 %convolution_convert_fusion = bf16[8,1536,1024]{2,1,0:T(8,128)(2,1)} fusion(bf16[8,8,8,1024]{3,2,1,0:T(8,128)(2,1)S(1)} %bitcast.66, bf16[8,64,1536]{2,1,0:T(8,128)(2,1)S(1)} %copy-done.2, bf16[8,64,1536]{2,1,0:T(8,128)(2,1)} %get-tuple-element.6), kind=kOutput, calls=%fused_computation | convolution fusion | flops 1629487104 | bytes 29360128 | tf_op jit(solution)/shard_map/erf,erd->efd/dot_general | solution.py:51
  304.8 1.9 copy.53
  306.6 1.2 convolution_convert_fusion.8
  307.9 9.8 %all-to-all-done.3 = bf16[8,64,1024]{2,0,1:T(8,128)(2,1)} async-done(((bf16[8,64,1024]{2,0,1:T(8,128)(2,1)}), bf16[8,64,1024]{2,0,1:T(8,128)(2,1)}, u32[]{:S(2)}, u32[]{:S(2)}) %all-to-all-start.3) | async-done | bytes 1048608 | tf_op jit(solution)/shard_map/all_to_all | solution.py:73
  317.6 1.8 copy.57
  319.5 0.9 convolution_convert_fusion.7
  (22 shorter events, 0.2 us)
Async XLA Ops:
  7.2 3.9 %copy-start = (bf16[32,1024]{1,0:T(8,128)(2,1)S(1)}, bf16[32,1024]{1,0:T(8,128)(2,1)}, u32[]{:S(2)}) copy-start(bf16[32,1024]{1,0:T(8,128)(2,1)} %param.7) | copy-start | bytes 196612
  7.2 11.6 %copy-start.6 = (bf16[32,1024]{1,0:T(8,128)(2,1)S(1)}, bf16[32,1024]{1,0:T(8,128)(2,1)}, u32[]{:S(2)}) copy-start(bf16[32,1024]{1,0:T(8,128)(2,1)} %param.8) | copy-start | bytes 196612
  10.4 0.6 copy-start.4
  12.4 32.9 %all-to-all-start = ((bf16[64,8,1024]{2,1,0:T(8,128)(2,1)}), bf16[64,8,1024]{2,1,0:T(8,128)(2,1)S(1)}, u32[]{:S(2)}, u32[]{:S(2)}) async-start(bf16[64,8,1024]{2,1,0:T(8,128)(2,1)} %fusion), calls=%async_computation | async-start | bytes 2097152 | tf_op jit(solution)/shard_map/all_to_all | solution.py:36
  45.4 31.1 %all-to-all-start.2 = ((bf16[64,8,1024]{2,1,0:T(8,128)(2,1)}), bf16[64,8,1024]{2,1,0:T(8,128)(2,1)S(1)}, u32[]{:S(2)}, u32[]{:S(2)}) async-start(bf16[64,8,1024]{2,1,0:T(8,128)(2,1)} %fusion.1), calls=%async_computation.2 | async-start | bytes 2097152 | tf_op jit(solution)/shard_map/all_to_all | solution.py:37
  48.9 116.0 %all-reduce.3.cloned.1.call-start = ((), (), s32[]{:S(2)}) async-start(), calls=%async_computation.8 | async-start | bytes 6291456 | tf_op jit(solution)/shard_map/psum | solution.py:43
  76.4 122.6 %reduce-scatter.4.cloned.1.call-start = ((), (), s32[]{:S(2)}) async-start(), calls=%async_computation.7 | async-start | bytes 1966080
  98.6 138.5 %all-gather.3.cloned.1.call-start = ((), (), s32[]{:S(2)}) async-start(), calls=%async_computation.5 | async-start | bytes 1966080 | tf_op jit(solution)/shard_map/all_gather | solution.py:64
  164.9 3.6 %copy-start.2 = (bf16[8,64,1536]{2,1,0:T(8,128)(2,1)S(1)}, bf16[8,64,1536]{2,1,0:T(8,128)(2,1)}, u32[]{:S(2)}) copy-start(bf16[8,64,1536]{2,1,0:T(8,128)(2,1)} %get-tuple-element.5) | copy-start | bytes 4718596
  201.8 1.9 copy-start.3
  206.3 63.3 %all-gather.5.cloned.1.call-start = ((), (), s32[]{:S(2)}) async-start(), calls=%async_computation.6 | async-start | bytes 1966080 | tf_op jit(solution)/shard_map/all_gather | solution.py:65
  222.0 64.3 %all-to-all-start.1 = ((bf16[8,64,1024]{2,0,1:T(8,128)(2,1)}), bf16[8,64,1024]{2,0,1:T(8,128)(2,1)}, u32[]{:S(2)}, u32[]{:S(2)}) async-start(bf16[8,64,1024]{2,0,1:T(8,128)(2,1)} %copy.51), calls=%async_computation.1 | async-start | bytes 2097152 | tf_op jit(solution)/shard_map/all_to_all | solution.py:72
  286.3 31.3 %all-to-all-start.3 = ((bf16[8,64,1024]{2,0,1:T(8,128)(2,1)}), bf16[8,64,1024]{2,0,1:T(8,128)(2,1)}, u32[]{:S(2)}, u32[]{:S(2)}) async-start(bf16[8,64,1024]{2,0,1:T(8,128)(2,1)} %copy.55), calls=%async_computation.3 | async-start | bytes 2097152 | tf_op jit(solution)/shard_map/all_to_all | solution.py:73
  304.8 14.7 %copy-start.5 = (bf16[32,512]{1,0:T(8,128)(2,1)S(1)}, bf16[32,512]{1,0:T(8,128)(2,1)}, u32[]{:S(2)}) copy-start(bf16[32,512]{1,0:T(8,128)(2,1)} %copy-done.4) | copy-start | bytes 98308
  304.8 15.6 %copy-start.1 = (bf16[32,1024]{1,0:T(8,128)(2,1)S(1)}, bf16[32,1024]{1,0:T(8,128)(2,1)}, u32[]{:S(2)}) copy-start(bf16[32,1024]{1,0:T(8,128)(2,1)} %param.7) | copy-start | bytes 196612
Sparse Core Ops, SparseCore 0:
  76.5 88.3 all-reduce.2
  167.9 31.1 reduce-scatter.3
  206.4 30.6 all-gather.2
  238.8 30.6 all-gather.4
where the time goes:
time: 328 us; the launch traced here: 327 us
  waiting for transfers between devices  158 us (48%)
  matrix products  101 us (31%)
  local copies, waits for them, and re-layouts  22.4 us (7%)
  starting transfers between devices  19.4 us (6%)
  between operations  13.9 us (4%)
  other arithmetic  11.7 us (4%)
    psum x1, waiting for transfers between devices, local(): lax.psum(pre_gate.astype(jnp.bfloat16), 'tensor').astype(jnp.float32)  66 us
    unnamed x5, waiting for transfers between devices  28.6 us
    all_to_all x1, waiting for transfers between devices, local(): lax.all_to_all(token_send, 'expert', split_axis=0, concat_axis=1, tiled=T...  24.5 us
    all_gather x1, waiting for transfers between devices, local(): up_piece = lax.all_gather(up_grad, 'tensor', axis=2, tiled=True)  18.6 us
    dot_general x1, matrix products, local(): jnp.einsum('erf,edf->erd', up_piece, w_up, preferred_element_type=jnp.flo...  14 us
    unnamed x20, local copies, waits for them, and re-layouts  13.9 us
    dot_general x1, matrix products, local(): jnp.einsum('erf,erd->efd', hidden, grad_rows, preferred_element_type=jnp....  13.8 us
    dot_general x1, matrix products, local(): jnp.einsum('erf,edf->erd', gate_piece, w_gate, preferred_element_type=jnp...  13.8 us
  transfers between devices with their start and end apart: 8, of which 6 were waited for; matrix products, arithmetic and copies ran while one was open for 37% of the time, Pallas kernels for 0%

commit v1 on v0

--- a/solution.py
+++ b/solution.py
@@ -33,7 +33,12 @@
         experts, capacity, model_width
     )
     token_rows, grad_rows = (
-        lax.all_to_all(token_send, "expert", split_axis=0, concat_axis=1, tiled=True),
+        jnp.concatenate(
+            lax.all_to_all(
+                jnp.stack(jnp.split(token_send, lax.axis_size("expert"), axis=0)), "expert", 0, 0
+            ),
+            axis=1,
+        ),
         lax.all_to_all(gradient_outgoing, "expert", split_axis=0, concat_axis=1, tiled=True),
     )
     pre_gate = jnp.einsum("erd,edf->erf", token_rows, w_gate, preferred_element_type=jnp.float32)

time: 328 us -> 332 us (1.012)
  local copies, waits for them, and re-layouts: 22.4 us -> 27.7 us
    unnamed x20 -> x27, local copies, waits for them, and re-layouts: 13.9 us -> 18.5 us
  transfers between devices with their start and end apart: 8 -> 8, of which waited for: 6 -> 6; matrix products, arithmetic and copies ran while one was open for 37% -> 36% of each run, Pallas kernels for 0% -> 0%
where the time goes in v1:
time: 332 us; the launch traced here: 331 us
  waiting for transfers between devices  158 us (48%)
  matrix products  100 us (30%)
  local copies, waits for them, and re-layouts  27.7 us (8%)
  starting transfers between devices  19.4 us (6%)
  between operations  13.9 us (4%)
  other arithmetic  11.7 us (4%)
    psum x1, waiting for transfers between devices, local(): lax.psum(pre_gate.astype(jnp.bfloat16), 'tensor').astype(jnp.float32)  66 us
    unnamed x5, waiting for transfers between devices  28.6 us
    all_to_all x1, waiting for transfers between devices, local(): lax.all_to_all(jnp.stack(jnp.split(token_send, lax.axis_size('expert'), a...  24.5 us
    all_gather x1, waiting for transfers between devices, local(): up_piece = lax.all_gather(up_grad, 'tensor', axis=2, tiled=True)  18.6 us
    unnamed x27, local copies, waits for them, and re-layouts  18.5 us
    dot_general x1, matrix products, local(): jnp.einsum('erf,edf->erd', up_piece, w_up, preferred_element_type=jnp.flo...  14 us
    dot_general x1, matrix products, local(): jnp.einsum('erf,erd->efd', hidden, grad_rows, preferred_element_type=jnp....  13.8 us
    dot_general x1, matrix products, local(): jnp.einsum('erf,edf->erd', gate_piece, w_gate, preferred_element_type=jnp...  13.8 us
  transfers between devices with their start and end apart: 8, of which 6 were waited for; matrix products, arithmetic and copies ran while one was open for 36% of the time, Pallas kernels for 0%

profile of v1, /device:TPU:0, one launch (start us, length us, event | category | flops | bytes accessed | tf_op | source)
XLA Modules:
  0.0 331.3 jit_solution(13904371478443951147)
XLA Ops:
  7.2 0.8 copy.45
  8.2 0.8 copy.49
  8.9 0.6 reduce-window.6
  10.0 0.4 convert_reduce_fusion
  10.4 0.6 copy-done.4
  11.0 0.5 convolution_convert_fusion.6
  11.5 0.7 fusion.21
  12.1 0.7 fusion.20
  12.8 0.7 fusion.19
  13.5 0.7 fusion.18
  14.1 0.7 fusion.17
  14.8 0.7 fusion.16
  15.5 0.7 fusion.15
  16.1 0.7 fusion.14
  16.8 6.3 %all-to-all-start = ((bf16[8,8,8,1024]{3,2,1,0:T(8,128)(2,1)}), bf16[8,8,8,1024]{3,2,1,0:T(8,128)(2,1)S(1)}, u32[]{:S(2)}, u32[]{:S(2)}) async-start(bf16[8,8,8,1024]{3,2,1,0:T(8,128)(2,1)} %fusion.14), calls=%async_computation | async-start | bytes 2097152 | tf_op jit(solution)/shard_map/all_to_all | solution.py:37
  23.2 2.0 fusion
  25.2 24.5 %all-to-all-done = bf16[8,8,8,1024]{3,2,1,0:T(8,128)(2,1)S(1)} async-done(((bf16[8,8,8,1024]{3,2,1,0:T(8,128)(2,1)}), bf16[8,8,8,1024]{3,2,1,0:T(8,128)(2,1)S(1)}, u32[]{:S(2)}, u32[]{:S(2)}) %all-to-all-start) | async-done | bytes 1048608 | tf_op jit(solution)/shard_map/all_to_all | solution.py:37
  49.7 3.6 %all-to-all-start.2 = ((bf16[64,8,1024]{2,1,0:T(8,128)(2,1)}), bf16[64,8,1024]{2,1,0:T(8,128)(2,1)S(1)}, u32[]{:S(2)}, u32[]{:S(2)}) async-start(bf16[64,8,1024]{2,1,0:T(8,128)(2,1)} %fusion), calls=%async_computation.2 | async-start | bytes 2097152 | tf_op jit(solution)/shard_map/all_to_all | solution.py:42
  53.3 13.7 %convolution_convert_fusion.2 = bf16[8,64,1536]{2,1,0:T(8,128)(2,1)} fusion(bf16[8,1024,1536]{2,1,0:T(8,128)(2,1)} %param.12, bf16[8,8,8,1024]{3,2,1,0:T(8,128)(2,1)S(1)} %all-to-all-done), kind=kOutput, calls=%fused_computation.4 | convolution fusion | flops 1611399168 | bytes 27787264 | tf_op jit(solution)/shard_map/erd,edf->erf/dot_general | solution.py:45
  67.0 13.7 %convolution_convert_fusion.3 = bf16[8,64,1536]{2,1,0:T(8,128)(2,1)} fusion(bf16[8,1024,1536]{2,1,0:T(8,128)(2,1)} %param.11, bf16[8,8,8,1024]{3,2,1,0:T(8,128)(2,1)S(1)} %all-to-all-done), kind=kOutput, calls=%fused_computation.5 | convolution fusion | flops 1611399168 | bytes 27787264 | tf_op jit(solution)/shard_map/erd,edf->erf/dot_general | solution.py:44
  80.8 0.2 reduce-scatter.4.cloned.1.call-start
  81.0 13.2 %convolution_convert_fusion.1 = bf16[8,64,1536]{2,1,0:T(8,128)(2,1)S(1)} fusion(bf16[8,1536,1024]{2,1,0:T(8,128)(2,1)} %param.13, bf16[8,8,8,1024]{3,2,1,0:T(8,128)(2,1)S(1)} %bitcast.99), kind=kOutput, calls=%fused_computation.3 | convolution fusion | flops 1611399168 | bytes 27787264 | tf_op jit(solution)/shard_map/erd,efd->erf/dot_general | solution.py:61
  94.2 3.5 %copy.60 = bf16[8,64,1536]{1,0,2:T(8,128)(2,1)} copy(bf16[8,64,1536]{2,1,0:T(8,128)(2,1)S(1)} %convolution_convert_fusion.1) | data formatting | bytes 3145728
  97.7 5.4 %reshape.82 = bf16[1536,512]{1,0:T(8,128)(2,1)} reshape(bf16[1536,8,64]{2,1,0:T(8,128)(2,1)} %bitcast.101) | data formatting | bytes 3145728
  103.2 66.0 %all-reduce.3.cloned.1.call-done = (bf16[8,64,1536]{2,1,0:T(8,128)(2,1)}, bf16[8,64,1536]{2,1,0:T(8,128)(2,1)}) async-done(((bf16[8,64,1536]{2,1,0:T(8,128)(2,1)}, bf16[8,64,1536]{2,1,0:T(8,128)(2,1)}), (bf16[8,64,1536]{2,1,0:T(8,128)(2,1)}, bf16[8,64,1536]{2,1,0:T(8,128)(2,1)})) %all-reduce.3.cloned.1.call-update) | async-done | bytes 3145744 | tf_op jit(solution)/shard_map/psum | solution.py:48
  169.2 3.6 %convert_element_type.70 = f32[8,64,1536]{2,1,0:T(8,128)} convert(bf16[8,64,1536]{2,1,0:T(8,128)(2,1)} %get-tuple-element.5) | non-fusion elementwise | flops 786432 | bytes 4718592 | tf_op jit(solution)/shard_map/convert_element_type | solution.py:48
  172.8 2.5 add_divide_fusion
  175.3 28.1 %reduce-scatter.4.cloned.1.call-done = bf16[384,512]{1,0:T(8,128)(2,1)} async-done(((bf16[1536,512]{1,0:T(8,128)(2,1)}), bf16[384,512]{1,0:T(8,128)(2,1)}) %reduce-scatter.4.cloned.1.call-update) | async-done | bytes 393232
  203.4 1.5 reshape.83
  204.9 1.3 copy.61
  206.2 1.8 convert_element_type.72
  208.1 2.6 fusion.13
  210.7 0.5 all-gather.5.cloned.1.call-update
  211.2 13.5 %convolution_convert_fusion.4 = bf16[8,64,1024]{2,1,0:T(8,128)(2,1)S(1)} fusion(bf16[8,1536,1024]{2,1,0:T(8,128)(2,1)} %param.13, bf16[8,64,1536]{2,1,0:T(8,128)(2,1)S(1)} %copy-done.2, bf16[8,64,1536]{2,1,0:T(8,128)(2,1)} %get-tuple-element.6), kind=kOutput, calls=%fused_computation.7 | convolution fusion | flops 1617428480 | bytes 29360128 | tf_op jit(solution)/shard_map/erf,efd->erd/dot_general | solution.py:53
  224.8 1.6 copy.51
  226.4 4.6 %all-to-all-start.1 = ((bf16[8,64,1024]{2,0,1:T(8,128)(2,1)}), bf16[8,64,1024]{2,0,1:T(8,128)(2,1)}, u32[]{:S(2)}, u32[]{:S(2)}) async-start(bf16[8,64,1024]{2,0,1:T(8,128)(2,1)} %copy.51), calls=%async_computation.1 | async-start | bytes 2097152 | tf_op jit(solution)/shard_map/all_to_all | solution.py:77
  230.9 10.6 %all-gather.3.cloned.1.call-done = bf16[8,64,1536]{2,1,0:T(8,128)(2,1)} async-done(((bf16[8,64,384]{2,1,0:T(8,128)(2,1)}), bf16[8,64,1536]{2,1,0:T(8,128)(2,1)}) %all-gather.3.cloned.1.call-update) | async-done | bytes 1572880 | tf_op jit(solution)/shard_map/all_gather | solution.py:69
  241.5 13.8 %fusion.28 = f32[8,64,1024]{2,1,0:T(8,128)} fusion(bf16[8,64,1536]{2,1,0:T(8,128)(2,1)} %all-gather.3.cloned.1.call-done, bf16[8,1024,1536]{2,1,0:T(8,128)(2,1)} %param.11), kind=kOutput, calls=%fused_computation.59 | convolution fusion | flops 1610612736 | bytes 28835840 | tf_op jit(solution)/shard_map/erf,edf->erd/dot_general | solution.py:71
  255.3 18.6 %all-gather.5.cloned.1.call-done = bf16[8,64,1536]{2,1,0:T(8,128)(2,1)} async-done(((bf16[8,64,384]{2,1,0:T(8,128)(2,1)}), bf16[8,64,1536]{2,1,0:T(8,128)(2,1)}) %all-gather.5.cloned.1.call-update) | async-done | bytes 1572880 | tf_op jit(solution)/shard_map/all_gather | solution.py:70
  273.9 14.0 %add_convert_fusion = bf16[8,64,1024]{2,1,0:T(8,128)(2,1)} fusion(f32[8,64,1024]{2,1,0:T(8,128)} %fusion.28, bf16[8,64,1536]{2,1,0:T(8,128)(2,1)} %all-gather.5.cloned.1.call-done, bf16[8,1024,1536]{2,1,0:T(8,128)(2,1)} %param.12), kind=kOutput, calls=%fused_computation.6 | convolution fusion | flops 1611661312 | bytes 29884416 | tf_op jit(solution)/shard_map/erf,edf->erd/dot_general | solution.py:72
  287.9 2.8 copy.55
  290.7 4.6 %all-to-all-start.3 = ((bf16[8,64,1024]{2,0,1:T(8,128)(2,1)}), bf16[8,64,1024]{2,0,1:T(8,128)(2,1)}, u32[]{:S(2)}, u32[]{:S(2)}) async-start(bf16[8,64,1024]{2,0,1:T(8,128)(2,1)} %copy.55), calls=%async_computation.3 | async-start | bytes 2097152 | tf_op jit(solution)/shard_map/all_to_all | solution.py:78
  295.3 13.8 %convolution_convert_fusion = bf16[8,1536,1024]{2,1,0:T(8,128)(2,1)} fusion(bf16[8,8,8,1024]{3,2,1,0:T(8,128)(2,1)S(1)} %bitcast.100, bf16[8,64,1536]{2,1,0:T(8,128)(2,1)S(1)} %copy-done.2, bf16[8,64,1536]{2,1,0:T(8,128)(2,1)} %get-tuple-element.6), kind=kOutput, calls=%fused_computation | convolution fusion | flops 1629487104 | bytes 29360128 | tf_op jit(solution)/shard_map/erf,erd->efd/dot_general | solution.py:56
  309.1 1.9 copy.53
  311.0 1.2 convolution_convert_fusion.8
  312.2 9.8 %all-to-all-done.3 = bf16[8,64,1024]{2,0,1:T(8,128)(2,1)} async-done(((bf16[8,64,1024]{2,0,1:T(8,128)(2,1)}), bf16[8,64,1024]{2,0,1:T(8,128)(2,1)}, u32[]{:S(2)}, u32[]{:S(2)}) %all-to-all-start.3) | async-done | bytes 1048608 | tf_op jit(solution)/shard_map/all_to_all | solution.py:78
  322.0 1.8 copy.57
  323.8 0.9 convolution_convert_fusion.7
  (30 shorter events, 0.8 us)
Async XLA Ops:
  7.2 3.9 %copy-start = (bf16[32,1024]{1,0:T(8,128)(2,1)S(1)}, bf16[32,1024]{1,0:T(8,128)(2,1)}, u32[]{:S(2)}) copy-start(bf16[32,1024]{1,0:T(8,128)(2,1)} %param.7) | copy-start | bytes 196612
  7.2 16.0 %copy-start.6 = (bf16[32,1024]{1,0:T(8,128)(2,1)S(1)}, bf16[32,1024]{1,0:T(8,128)(2,1)}, u32[]{:S(2)}) copy-start(bf16[32,1024]{1,0:T(8,128)(2,1)} %param.8) | copy-start | bytes 196612
  10.4 0.6 copy-start.4
  16.8 32.9 %all-to-all-start = ((bf16[8,8,8,1024]{3,2,1,0:T(8,128)(2,1)}), bf16[8,8,8,1024]{3,2,1,0:T(8,128)(2,1)S(1)}, u32[]{:S(2)}, u32[]{:S(2)}) async-start(bf16[8,8,8,1024]{3,2,1,0:T(8,128)(2,1)} %fusion.14), calls=%async_computation | async-start | bytes 2097152 | tf_op jit(solution)/shard_map/all_to_all | solution.py:37
  49.7 31.3 %all-to-all-start.2 = ((bf16[64,8,1024]{2,1,0:T(8,128)(2,1)}), bf16[64,8,1024]{2,1,0:T(8,128)(2,1)S(1)}, u32[]{:S(2)}, u32[]{:S(2)}) async-start(bf16[64,8,1024]{2,1,0:T(8,128)(2,1)} %fusion), calls=%async_computation.2 | async-start | bytes 2097152 | tf_op jit(solution)/shard_map/all_to_all | solution.py:42
  53.3 116.0 %all-reduce.3.cloned.1.call-start = ((), (), s32[]{:S(2)}) async-start(), calls=%async_computation.8 | async-start | bytes 6291456 | tf_op jit(solution)/shard_map/psum | solution.py:48
  80.8 122.6 %reduce-scatter.4.cloned.1.call-start = ((), (), s32[]{:S(2)}) async-start(), calls=%async_computation.7 | async-start | bytes 1966080
  103.1 138.4 %all-gather.3.cloned.1.call-start = ((), (), s32[]{:S(2)}) async-start(), calls=%async_computation.5 | async-start | bytes 1966080 | tf_op jit(solution)/shard_map/all_gather | solution.py:69
  169.2 3.6 %copy-start.2 = (bf16[8,64,1536]{2,1,0:T(8,128)(2,1)S(1)}, bf16[8,64,1536]{2,1,0:T(8,128)(2,1)}, u32[]{:S(2)}) copy-start(bf16[8,64,1536]{2,1,0:T(8,128)(2,1)} %get-tuple-element.5) | copy-start | bytes 4718596
  206.2 1.9 copy-start.3
  210.7 63.3 %all-gather.5.cloned.1.call-start = ((), (), s32[]{:S(2)}) async-start(), calls=%async_computation.6 | async-start | bytes 1966080 | tf_op jit(solution)/shard_map/all_gather | solution.py:70
  226.4 64.3 %all-to-all-start.1 = ((bf16[8,64,1024]{2,0,1:T(8,128)(2,1)}), bf16[8,64,1024]{2,0,1:T(8,128)(2,1)}, u32[]{:S(2)}, u32[]{:S(2)}) async-start(bf16[8,64,1024]{2,0,1:T(8,128)(2,1)} %copy.51), calls=%async_computation.1 | async-start | bytes 2097152 | tf_op jit(solution)/shard_map/all_to_all | solution.py:77
  290.7 31.3 %all-to-all-start.3 = ((bf16[8,64,1024]{2,0,1:T(8,128)(2,1)}), bf16[8,64,1024]{2,0,1:T(8,128)(2,1)}, u32[]{:S(2)}, u32[]{:S(2)}) async-start(bf16[8,64,1024]{2,0,1:T(8,128)(2,1)} %copy.55), calls=%async_computation.3 | async-start | bytes 2097152 | tf_op jit(solution)/shard_map/all_to_all | solution.py:78
  309.1 14.7 %copy-start.5 = (bf16[32,512]{1,0:T(8,128)(2,1)S(1)}, bf16[32,512]{1,0:T(8,128)(2,1)}, u32[]{:S(2)}) copy-start(bf16[32,512]{1,0:T(8,128)(2,1)} %copy-done.4) | copy-start | bytes 98308
  309.1 15.6 %copy-start.1 = (bf16[32,1024]{1,0:T(8,128)(2,1)S(1)}, bf16[32,1024]{1,0:T(8,128)(2,1)}, u32[]{:S(2)}) copy-start(bf16[32,1024]{1,0:T(8,128)(2,1)} %param.7) | copy-start | bytes 196612
Sparse Core Ops, SparseCore 0:
  80.9 88.3 all-reduce.2
  172.2 31.1 reduce-scatter.3
  210.8 30.6 all-gather.2
  243.2 30.6 all-gather.4
